TPU v7x, 512 devices: a whole 4x8x8 slice. The times are simulated.
512 devices in a mesh: row: 32 (over x, y), col: 16 (over z, core).
Axes of the slice: x: 4, y: 8, z: 8, core: 2. Of those that a mesh axis runs over, the one named last changes fastest.
Arguments:
- points_here: float32 [4, 3, 128, 256, 128], P(None, None, 'row', 'col'), may hold values from -4 to 4
- points_there: float32 [4, 3, 128, 256, 128], P(None, None, 'row', 'col'), may hold values from -4 to 4
- outlier_mask: int32 [4, 128, 256, 128], P(None, 'row', 'col'), may hold values 0 or 1
- transforms: float32 [3, 4, 128, 256], P(None, None, 'row', 'col'), may hold values from -3 to 3
Outputs:
- aligned: float32 [3, 4, 128, 256], P(None, None, 'row', 'col')
- error_stats: float32 [2, 2], replicated
All inputs are finite; a program needn't handle non-finite values. No bound on the sum of `outlier_mask` on one device may be relied on, other than what follows from the above.
Results may differ from a plain program's by a relative error of at most 0.0003.
Values sent between devices are 32-bit elements; how exact they have to be, the bound alone decides.
A program may use at most 64 MiB of HBM per device.

v0:
```python
import jax
import jax.numpy as jnp
from jax import lax
from jax.sharding import Mesh
from jax.sharding import PartitionSpec as P

ITERS = 2
COL = ("col_0", "col_1")
ROW = ("row_0", "row_1")
ROW_COL = ("row_0", "row_1", "col_0", "col_1")


link_offsets = ((0, 1), (1, 0), (1, 1), (1, -1))
damping_scale = 64.0


def from_behind(array, axis, by):
    peers = lax.axis_size(axis)
    pairs = [(i, i + by) for i in range(peers) if 0 <= i + by < peers]
    return lax.ppermute(array, axis, pairs)


def with_halo(block, sides, width):
    for axis, dim in sides:
        count = lax.axis_size(axis)
        forward = [(i, i + 1) for i in range(count - 1)]
        backward = [(target, source) for source, target in forward]
        low = lax.ppermute(
            lax.slice_in_dim(block, block.shape[dim] - width, None, axis=dim), axis, forward
        )
        high = lax.ppermute(lax.slice_in_dim(block, 0, width, axis=dim), axis, backward)
        block = jnp.concatenate([low, block, high], axis=dim)
    return block


def joined_all(array, axes, combine):
    for axis in axes:
        pieces = jax.tree.map(lambda part: lax.all_gather(part, axis), array)
        array = jax.tree.map(lambda part: part[0], pieces)
        for k in range(1, lax.axis_size(axis)):
            array = combine(array, jax.tree.map(lambda part: part[k], pieces))
    return array


def apply_affine(affine, points):
    mapped = []
    for component in range(3):
        value = affine[component, 3][..., None] + affine[component, 0][..., None] * points[0]
        value = value + affine[component, 1][..., None] * points[1]
        value = value + affine[component, 2][..., None] * points[2]
        mapped.append(value)
    return jnp.stack(mapped)


def link_error(here, there):
    delta = here - there
    return delta[0] * delta[0] + delta[1] * delta[1] + delta[2] * delta[2]


def gram_terms(weight, points):
    weighted = [weight * points[0], weight * points[1], weight * points[2], weight]
    entries = []
    for first in range(4):
        for second in range(4):
            if second == 3:
                entries.append(jnp.sum(weighted[first], axis=-1))
            else:
                entries.append(jnp.sum(weighted[first] * points[second], axis=-1))
    return jnp.stack(entries).reshape((4, 4) + weight.shape[:-1])


def cross_terms(weight, target, points):
    entries = []
    for component in range(3):
        scaled = weight * target[component]
        for second in range(4):
            if second == 3:
                entries.append(jnp.sum(scaled, axis=-1))
            else:
                entries.append(jnp.sum(scaled * points[second], axis=-1))
    return jnp.stack(entries).reshape((3, 4) + weight.shape[:-1])


def solve_small(gram, rhs):
    factor = [[None] * 4 for _ in range(4)]
    for first in range(4):
        for second in range(first + 1):
            value = gram[first, second]
            for inner in range(second):
                value = value - factor[first][inner] * factor[second][inner]
            if first == second:
                factor[first][first] = jnp.sqrt(value)
            else:
                factor[first][second] = value / factor[second][second]
    result = []
    for component in range(3):
        forward = []
        for first in range(4):
            value = rhs[component, first]
            for inner in range(first):
                value = value - factor[first][inner] * forward[inner]
            forward.append(value / factor[first][first])
        backward = [None] * 4
        for first in (3, 2, 1, 0):
            value = forward[first]
            for inner in range(first + 1, 4):
                value = value - factor[inner][first] * backward[inner]
            backward[first] = value / factor[first][first]
        result.append(jnp.stack(backward))
    return jnp.stack(result)


def combine_stats(earlier, later):
    return (jnp.maximum(earlier[0], later[0]), earlier[1] + later[1], earlier[2] + later[2])


def move_blocks(packages):
    east_pair = jnp.stack([packages[0], packages[2]])
    arrived_east = from_behind(east_pair[:, :, :, -1:], COL, 1)
    east_pair = jnp.concatenate([arrived_east, east_pair[:, :, :, :-1]], axis=3)
    west_one = packages[3]
    arrived_west = from_behind(west_one[:, :, :1], COL, -1)
    west_one = jnp.concatenate([west_one[:, :, 1:], arrived_west], axis=2)
    south_set = jnp.stack([packages[1], east_pair[1], west_one])
    arrived_south = from_behind(south_set[:, :, -1:], ROW, 1)
    south_set = jnp.concatenate([arrived_south, south_set[:, :, :-1]], axis=2)
    return [east_pair[0], south_set[0], south_set[1], south_set[2]]


def on_device(points_here, points_there, outlier_mask, transforms):
    rows_local = transforms.shape[2]
    cols_local = transforms.shape[3]
    grid_rows = rows_local * lax.axis_size(ROW)
    grid_cols = cols_local * lax.axis_size(COL)
    row_ids = lax.axis_index(ROW) * rows_local + jnp.arange(rows_local, dtype=jnp.int32)
    col_ids = lax.axis_index(COL) * cols_local + jnp.arange(cols_local, dtype=jnp.int32)
    weight_masks = []
    for direction in range(4):
        row_step, col_step = link_offsets[direction]
        row_valid = row_ids + row_step < grid_rows
        col_valid = (col_ids + col_step >= 0) & (col_ids + col_step < grid_cols)
        valid = (row_valid[:, None] & col_valid[None, :]).astype(jnp.float32)
        weight_masks.append(outlier_mask[direction].astype(jnp.float32) * valid[..., None])
    affine = transforms
    records = []
    for iteration in range(ITERS):
        side_ext = with_halo(affine, ((COL, 3),), 1)
        below = from_behind(side_ext[:, :, :1], ROW, -1)
        extended = jnp.concatenate([side_ext, below], axis=2)
        mapped_here = []
        mapped_there = []
        errors = []
        largest_local = jnp.zeros((), jnp.float32)
        total_local = jnp.zeros((), jnp.float32)
        count_local = jnp.zeros((), jnp.float32)
        for direction in range(4):
            row_step, col_step = link_offsets[direction]
            target = extended[
                :, :, row_step : row_step + rows_local, 1 + col_step : 1 + col_step + cols_local
            ]
            here = apply_affine(affine, points_here[direction])
            there = apply_affine(target, points_there[direction])
            error = link_error(here, there)
            masked = weight_masks[direction] * error
            largest_local = jnp.maximum(largest_local, jnp.max(masked))
            total_local = total_local + jnp.sum(masked)
            count_local = count_local + jnp.sum(weight_masks[direction])
            mapped_here.append(here)
            mapped_there.append(there)
            errors.append(error)
        largest, total, count = joined_all(
            (largest_local, total_local, count_local), ROW_COL, combine_stats
        )
        mean_error = total / jnp.maximum(count, 1.0)
        scale = 0.25 * largest + 1e-06
        damping = damping_scale * mean_error + 1.0
        gram = jnp.zeros((4, 4, rows_local, cols_local), jnp.float32)
        cross = jnp.zeros((3, 4, rows_local, cols_local), jnp.float32)
        packages = []
        for direction in range(4):
            weight = weight_masks[direction] / (1.0 + errors[direction] / scale)
            gram = gram + gram_terms(weight, points_here[direction])
            cross = cross + cross_terms(weight, mapped_there[direction], points_here[direction])
            far_gram = gram_terms(weight, points_there[direction]).reshape(
                (16, rows_local, cols_local)
            )
            far_cross = cross_terms(
                weight, mapped_here[direction], points_there[direction]
            ).reshape((12, rows_local, cols_local))
            packages.append(jnp.concatenate([far_gram, far_cross], axis=0))
        arrived = move_blocks(packages)
        for package in arrived:
            gram = gram + package[:16].reshape((4, 4, rows_local, cols_local))
            cross = cross + package[16:].reshape((3, 4, rows_local, cols_local))
        identity = jnp.eye(4, dtype=jnp.float32)[:, :, None, None]
        affine = solve_small(gram + damping * identity, cross + damping * affine)
        records.append(jnp.stack([largest, mean_error]))
    return (affine, jnp.stack(records, axis=1))


def solution(mesh):
    finer = Mesh(mesh.devices.reshape(4, 8, 8, 2), ("row_0", "row_1", "col_0", "col_1"))
    placed = (
        P(None, None, ROW, COL, None),
        P(None, None, ROW, COL, None),
        P(None, ROW, COL, None),
        P(None, None, ROW, COL),
    )
    return jax.shard_map(
        on_device,
        mesh=finer,
        in_specs=placed,
        out_specs=(P(None, None, ROW, COL), P()),
        check_vma=False,
    )
```

profile of v0, /device:TPU:66, one launch (start us, length us, event | category | flops | bytes accessed | tf_op | source)
XLA Modules:
  0.0 216.4 jit_solution(15908432011982294063)
XLA Ops:
  1.6 2.0 collective-permute-start
  3.6 2.4 %collective-permute-start.1 = (f32[3,4,4,1]{3,2,1,0:T(4,128)S(1)}, f32[3,4,4,1]{3,2,1,0:T(4,128)S(1)}, u32[]{:S(2)}, u32[]{:S(2)}) collective-permute-start(f32[3,4,4,1]{3,2,1,0:T(4,128)S(1)} %get-tuple-element.939), channel_id=1, source_target_pairs={{0,1},{1,2},{2,3},{3,4},{4,5},{5,6},{6,7},{7,8},{8,9},{9,10},{10,1... | collective-permute-start | bytes 584 | tf_op jit(solution)/shard_map/ppermute | solution.py:28
  8.9 5.3 %collective-permute-start.2 = (f32[3,4,1,18]{3,2,1,0:T(1,128)S(1)}, f32[3,4,1,18]{3,2,1,0:T(1,128)S(1)}, u32[]{:S(2)}, u32[]{:S(2)}) collective-permute-start(f32[3,4,1,18]{3,2,1,0:T(1,128)S(1)} %pad_maximum_fusion.33), channel_id=1, source_target_pairs={{16,0},{32,16},{48,32},{64,48},{80,64},{96,80},{112,96},{128,112},... | collective-permute-start | bytes 2600 | tf_op jit(solution)/shard_map/ppermute | solution.py:20
  31.1 9.6 %all-reduce.25 = (f32[4]{0:T(128)S(1)}, f32[4]{0:T(128)S(1)}, f32[4]{0:T(128)S(1)}) all-reduce(f32[4]{0:T(128)S(1)} %dynamic-update-slice, f32[4]{0:T(128)S(1)} %dynamic-update-slice.4, f32[4]{0:T(128)S(1)} %dynamic-update-slice.8), channel_id=1, replica_groups=mesh['row_0'=4,'row_1'=8,'col_0'=8,'col_1'=2] {'row_0'}, use_global_device_ids=true, to_apply=%add | all-reduce | flops 12 | bytes 96
  44.2 16.7 %all-reduce.23 = (f32[8]{0:T(128)S(1)}, f32[8]{0:T(128)S(1)}, f32[8]{0:T(128)S(1)}) all-reduce(f32[8]{0:T(128)S(1)} %maximum_dynamic-update-slice_fusion.5, f32[8]{0:T(128)S(1)} %add_dynamic-update-slice_fusion.8, f32[8]{0:T(128)S(1)} %add_dynamic-update-slice_fusion.7), channel_id=1, replica_groups=mesh['row_0'=4,'row_1'=8,'col_0'=8,'col_1'=2] {'row_1'}, use_global_device_ids=true, to_apply=%add.1 | all-reduce | flops 24 | bytes 192
  64.6 20.1 %all-reduce.21 = (f32[8]{0:T(128)S(1)}, f32[8]{0:T(128)S(1)}, f32[8]{0:T(128)S(1)}) all-reduce(f32[8]{0:T(128)S(1)} %maximum_dynamic-update-slice_fusion.3, f32[8]{0:T(128)S(1)} %add_dynamic-update-slice_fusion.5, f32[8]{0:T(128)S(1)} %add_dynamic-update-slice_fusion.3), channel_id=1, replica_groups=mesh['row_0'=4,'row_1'=8,'col_0'=8,'col_1'=2] {'col_0'}, use_global_device_ids=true, to_apply=%add.2 | all-reduce | flops 24 | bytes 192
  87.2 2.4 %all-reduce.27 = (f32[2]{0:T(128)S(1)}, f32[2]{0:T(128)S(1)}, f32[2]{0:T(128)S(1)}) all-reduce(f32[2]{0:T(128)S(1)} %maximum_dynamic-update-slice_fusion.2, f32[2]{0:T(128)S(1)} %add_dynamic-update-slice_fusion.4, f32[2]{0:T(128)S(1)} %add_dynamic-update-slice_fusion.2), channel_id=1, replica_groups=mesh['row_0'=4,'row_1'=8,'col_0'=8,'col_1'=2] {'col_1'}, use_global_device_ids=true, to_apply=%add.3 | all-reduce | flops 6 | bytes 48
  96.3 2.1 collective-permute-start.3
  99.8 4.2 %collective-permute-start.4 = (f32[28,4,1]{2,1,0:T(4,128)S(1)}, f32[28,4,1]{2,1,0:T(4,128)S(1)}, u32[]{:S(2)}, u32[]{:S(2)}) collective-permute-start(f32[28,4,1]{2,1,0:T(4,128)S(1)} %bitcast.4433), channel_id=1, source_target_pairs={{1,0},{2,1},{3,2},{4,3},{5,4},{6,5},{7,6},{8,7},{9,8},{10,9},{11,1... | collective-permute-start | bytes 1352 | tf_op jit(solution)/shard_map/ppermute | solution.py:20
  109.4 1.9 collective-permute-start.5
  111.5 5.9 %collective-permute-done.5 = f32[3,28,1,16]{3,2,1,0:T(1,128)S(1)} collective-permute-done((f32[3,28,1,16]{3,2,1,0:T(1,128)S(1)}, f32[3,28,1,16]{3,2,1,0:T(1,128)S(1)}, u32[]{:S(2)}, u32[]{:S(2)}) %collective-permute-start.5) | collective-permute-done | bytes 5408 | tf_op jit(solution)/shard_map/ppermute | solution.py:20
  118.0 1.9 collective-permute-start.6
  119.9 2.4 %collective-permute-start.7 = (f32[3,4,4,1]{3,2,1,0:T(4,128)S(1)}, f32[3,4,4,1]{3,2,1,0:T(4,128)S(1)}, u32[]{:S(2)}, u32[]{:S(2)}) collective-permute-start(f32[3,4,4,1]{3,2,1,0:T(4,128)S(1)} %get-tuple-element.926), channel_id=1, source_target_pairs={{0,1},{1,2},{2,3},{3,4},{4,5},{5,6},{6,7},{7,8},{8,9},{9,10},{10,1... | collective-permute-start | bytes 584 | tf_op jit(solution)/shard_map/ppermute | solution.py:28
  122.7 2.4 %collective-permute-done.7 = f32[3,4,4,1]{3,2,1,0:T(4,128)S(1)} collective-permute-done((f32[3,4,4,1]{3,2,1,0:T(4,128)S(1)}, f32[3,4,4,1]{3,2,1,0:T(4,128)S(1)}, u32[]{:S(2)}, u32[]{:S(2)}) %collective-permute-start.7) | collective-permute-done | bytes 224 | tf_op jit(solution)/shard_map/ppermute | solution.py:28
  125.1 2.1 collective-permute-start.8
  127.4 3.3 %collective-permute-done.8 = f32[3,4,1,18]{3,2,1,0:T(1,128)S(1)} collective-permute-done((f32[3,4,1,18]{3,2,1,0:T(1,128)S(1)}, f32[3,4,1,18]{3,2,1,0:T(1,128)S(1)}, u32[]{:S(2)}, u32[]{:S(2)}) %collective-permute-start.8) | collective-permute-done | bytes 896 | tf_op jit(solution)/shard_map/ppermute | solution.py:20
  139.3 7.0 %all-reduce.24 = (f32[4]{0:T(128)S(1)}, f32[4]{0:T(128)S(1)}) all-reduce(f32[4]{0:T(128)S(1)} %dynamic-update-slice.12, f32[4]{0:T(128)S(1)} %dynamic-update-slice.16), channel_id=1, replica_groups=mesh['row_0'=4,'row_1'=8,'col_0'=8,'col_1'=2] {'row_0'}, use_global_device_ids=true, to_apply=%add.12 | all-reduce | flops 8 | bytes 64
  147.8 17.5 %all-reduce.22 = (f32[8]{0:T(128)S(1)}, f32[8]{0:T(128)S(1)}) all-reduce(f32[8]{0:T(128)S(1)} %maximum_dynamic-update-slice_fusion.4, f32[8]{0:T(128)S(1)} %add_dynamic-update-slice_fusion.6), channel_id=1, replica_groups=mesh['row_0'=4,'row_1'=8,'col_0'=8,'col_1'=2] {'row_1'}, use_global_device_ids=true, to_apply=%add.13 | all-reduce | flops 16 | bytes 128
  166.9 15.2 %all-reduce.20 = (f32[8]{0:T(128)S(1)}, f32[8]{0:T(128)S(1)}) all-reduce(f32[8]{0:T(128)S(1)} %maximum_dynamic-update-slice_fusion.1, f32[8]{0:T(128)S(1)} %add_dynamic-update-slice_fusion.1), channel_id=1, replica_groups=mesh['row_0'=4,'row_1'=8,'col_0'=8,'col_1'=2] {'col_0'}, use_global_device_ids=true, to_apply=%add.14 | all-reduce | flops 16 | bytes 128
  183.8 2.4 %all-reduce.26 = (f32[2]{0:T(128)S(1)}, f32[2]{0:T(128)S(1)}) all-reduce(f32[2]{0:T(128)S(1)} %maximum_dynamic-update-slice_fusion, f32[2]{0:T(128)S(1)} %add_dynamic-update-slice_fusion), channel_id=1, replica_groups=mesh['row_0'=4,'row_1'=8,'col_0'=8,'col_1'=2] {'col_1'}, use_global_device_ids=true, to_apply=%add.15 | all-reduce | flops 4 | bytes 32
  196.1 2.7 %collective-permute-start.10 = (f32[28,4,1]{2,1,0:T(4,128)S(1)}, f32[28,4,1]{2,1,0:T(4,128)S(1)}, u32[]{:S(2)}, u32[]{:S(2)}) collective-permute-start(f32[28,4,1]{2,1,0:T(4,128)S(1)} %bitcast.4434), channel_id=1, source_target_pairs={{1,0},{2,1},{3,2},{4,3},{5,4},{6,5},{7,6},{8,7},{9,8},{10,9},{11,1... | collective-permute-start | bytes 1352 | tf_op jit(solution)/shard_map/ppermute | solution.py:20
  203.0 4.1 %collective-permute-done.9 = f32[2,28,4,1]{3,2,1,0:T(4,128)S(1)} collective-permute-done((f32[2,28,4,1]{3,2,1,0:T(4,128)S(1)}, f32[2,28,4,1]{3,2,1,0:T(4,128)S(1)}, u32[]{:S(2)}, u32[]{:S(2)}) %collective-permute-start.9) | collective-permute-done | bytes 928 | tf_op jit(solution)/shard_map/ppermute | solution.py:20
  207.3 1.9 collective-permute-start.11
  209.4 5.9 %collective-permute-done.11 = f32[3,28,1,16]{3,2,1,0:T(1,128)S(1)} collective-permute-done((f32[3,28,1,16]{3,2,1,0:T(1,128)S(1)}, f32[3,28,1,16]{3,2,1,0:T(1,128)S(1)}, u32[]{:S(2)}, u32[]{:S(2)}) %collective-permute-start.11) | collective-permute-done | bytes 5408 | tf_op jit(solution)/shard_map/ppermute | solution.py:20
  (641 shorter events, 52.9 us)
Async XLA Ops:
  0.6 5.4 %copy-start.3 = (f32[3,4,4,16]{3,2,1,0:T(4,128)S(1)}, f32[3,4,4,16]{3,2,1,0:T(4,128)}, u32[]{:S(2)}) copy-start(f32[3,4,4,16]{3,2,1,0:T(4,128)} %param.7) | copy-start | bytes 9220
  1.6 13.8 %copy-start = (f32[4,3,4,16,128]{4,3,2,1,0:T(8,128)S(1)}, f32[4,3,4,16,128]{4,3,2,1,0:T(8,128)}, u32[]{:S(2)}) copy-start(f32[4,3,4,16,128]{4,3,2,1,0:T(8,128)} %param.4) | copy-start | bytes 1179652
  1.6 6.0 %collective-permute-start = (f32[3,4,4,1]{3,2,1,0:T(4,128)S(1)}, f32[3,4,4,1]{3,2,1,0:T(4,128)S(1)}, u32[]{:S(2)}, u32[]{:S(2)}) collective-permute-start(f32[3,4,4,1]{3,2,1,0:T(4,128)S(1)} %get-tuple-element.940), channel_id=1, source_target_pairs={{1,0},{2,1},{3,2},{4,3},{5,4},{6,5},{7,6},{8,7},{9,8},{10,9},{11,1... | collective-permute-start | bytes 584 | tf_op jit(solution)/shard_map/ppermute | solution.py:31
  3.6 5.1 %collective-permute-start.1 = (f32[3,4,4,1]{3,2,1,0:T(4,128)S(1)}, f32[3,4,4,1]{3,2,1,0:T(4,128)S(1)}, u32[]{:S(2)}, u32[]{:S(2)}) collective-permute-start(f32[3,4,4,1]{3,2,1,0:T(4,128)S(1)} %get-tuple-element.939), channel_id=1, source_target_pairs={{0,1},{1,2},{2,3},{3,4},{4,5},{5,6},{6,7},{7,8},{8,9},{9,10},{10,1... | collective-permute-start | bytes 584 | tf_op jit(solution)/shard_map/ppermute | solution.py:28
  8.9 6.9 %collective-permute-start.2 = (f32[3,4,1,18]{3,2,1,0:T(1,128)S(1)}, f32[3,4,1,18]{3,2,1,0:T(1,128)S(1)}, u32[]{:S(2)}, u32[]{:S(2)}) collective-permute-start(f32[3,4,1,18]{3,2,1,0:T(1,128)S(1)} %pad_maximum_fusion.33), channel_id=1, source_target_pairs={{16,0},{32,16},{48,32},{64,48},{80,64},{96,80},{112,96},{128,112},... | collective-permute-start | bytes 2600 | tf_op jit(solution)/shard_map/ppermute | solution.py:20
  15.6 1.0 copy-start.1
  17.5 0.9 copy-start.2
  96.3 12.8 %collective-permute-start.3 = (f32[2,28,4,1]{3,2,1,0:T(4,128)S(1)}, f32[2,28,4,1]{3,2,1,0:T(4,128)S(1)}, u32[]{:S(2)}, u32[]{:S(2)}) collective-permute-start(f32[2,28,4,1]{3,2,1,0:T(4,128)S(1)} %slice_maximum_fusion.1), channel_id=1, source_target_pairs={{0,1},{1,2},{2,3},{3,4},{4,5},{5,6},{6,7},{7,8},{8,9},{9,10},{10,1... | collective-permute-start | bytes 2696 | tf_op jit(solution)/shard_map/ppermute | solution.py:20
  99.8 9.2 %collective-permute-start.4 = (f32[28,4,1]{2,1,0:T(4,128)S(1)}, f32[28,4,1]{2,1,0:T(4,128)S(1)}, u32[]{:S(2)}, u32[]{:S(2)}) collective-permute-start(f32[28,4,1]{2,1,0:T(4,128)S(1)} %bitcast.4433), channel_id=1, source_target_pairs={{1,0},{2,1},{3,2},{4,3},{5,4},{6,5},{7,6},{8,7},{9,8},{10,9},{11,1... | collective-permute-start | bytes 1352 | tf_op jit(solution)/shard_map/ppermute | solution.py:20
  109.4 8.0 %collective-permute-start.5 = (f32[3,28,1,16]{3,2,1,0:T(1,128)S(1)}, f32[3,28,1,16]{3,2,1,0:T(1,128)S(1)}, u32[]{:S(2)}, u32[]{:S(2)}) collective-permute-start(f32[3,28,1,16]{3,2,1,0:T(1,128)S(1)} %pad_maximum_fusion.5), channel_id=1, source_target_pairs={{0,16},{16,32},{32,48},{48,64},{64,80},{80,96},{96,112},{112,128},... | collective-permute-start | bytes 16136 | tf_op jit(solution)/shard_map/ppermute | solution.py:20
  118.0 4.7 %collective-permute-start.6 = (f32[3,4,4,1]{3,2,1,0:T(4,128)S(1)}, f32[3,4,4,1]{3,2,1,0:T(4,128)S(1)}, u32[]{:S(2)}, u32[]{:S(2)}) collective-permute-start(f32[3,4,4,1]{3,2,1,0:T(4,128)S(1)} %get-tuple-element.927), channel_id=1, source_target_pairs={{1,0},{2,1},{3,2},{4,3},{5,4},{6,5},{7,6},{8,7},{9,8},{10,9},{11,1... | collective-permute-start | bytes 584 | tf_op jit(solution)/shard_map/ppermute | solution.py:31
  119.9 5.1 %collective-permute-start.7 = (f32[3,4,4,1]{3,2,1,0:T(4,128)S(1)}, f32[3,4,4,1]{3,2,1,0:T(4,128)S(1)}, u32[]{:S(2)}, u32[]{:S(2)}) collective-permute-start(f32[3,4,4,1]{3,2,1,0:T(4,128)S(1)} %get-tuple-element.926), channel_id=1, source_target_pairs={{0,1},{1,2},{2,3},{3,4},{4,5},{5,6},{6,7},{7,8},{8,9},{9,10},{10,1... | collective-permute-start | bytes 584 | tf_op jit(solution)/shard_map/ppermute | solution.py:28
  125.1 5.5 %collective-permute-start.8 = (f32[3,4,1,18]{3,2,1,0:T(1,128)S(1)}, f32[3,4,1,18]{3,2,1,0:T(1,128)S(1)}, u32[]{:S(2)}, u32[]{:S(2)}) collective-permute-start(f32[3,4,1,18]{3,2,1,0:T(1,128)S(1)} %pad_maximum_fusion.29), channel_id=1, source_target_pairs={{16,0},{32,16},{48,32},{64,48},{80,64},{96,80},{112,96},{128,112},... | collective-permute-start | bytes 2600 | tf_op jit(solution)/shard_map/ppermute | solution.py:20
  196.1 6.8 %collective-permute-start.10 = (f32[28,4,1]{2,1,0:T(4,128)S(1)}, f32[28,4,1]{2,1,0:T(4,128)S(1)}, u32[]{:S(2)}, u32[]{:S(2)}) collective-permute-start(f32[28,4,1]{2,1,0:T(4,128)S(1)} %bitcast.4434), channel_id=1, source_target_pairs={{1,0},{2,1},{3,2},{4,3},{5,4},{6,5},{7,6},{8,7},{9,8},{10,9},{11,1... | collective-permute-start | bytes 1352 | tf_op jit(solution)/shard_map/ppermute | solution.py:20
  201.0 6.1 %collective-permute-start.9 = (f32[2,28,4,1]{3,2,1,0:T(4,128)S(1)}, f32[2,28,4,1]{3,2,1,0:T(4,128)S(1)}, u32[]{:S(2)}, u32[]{:S(2)}) collective-permute-start(f32[2,28,4,1]{3,2,1,0:T(4,128)S(1)} %slice_maximum_fusion), channel_id=1, source_target_pairs={{0,1},{1,2},{2,3},{3,4},{4,5},{5,6},{6,7},{7,8},{8,9},{9,10},{10,1... | collective-permute-start | bytes 2696 | tf_op jit(solution)/shard_map/ppermute | solution.py:20
  207.3 8.0 %collective-permute-start.11 = (f32[3,28,1,16]{3,2,1,0:T(1,128)S(1)}, f32[3,28,1,16]{3,2,1,0:T(1,128)S(1)}, u32[]{:S(2)}, u32[]{:S(2)}) collective-permute-start(f32[3,28,1,16]{3,2,1,0:T(1,128)S(1)} %pad_maximum_fusion.4), channel_id=1, source_target_pairs={{0,16},{16,32},{32,48},{48,64},{64,80},{80,96},{96,112},{112,128},... | collective-permute-start | bytes 16136 | tf_op jit(solution)/shard_map/ppermute | solution.py:20
where the time goes:
time: 218 us; the launch traced here: 216 us
  blocking collectives  91 us (42%)
  starting transfers between devices  30.9 us (14%)
  other arithmetic  30.1 us (14%)
  waiting for transfers between devices  22.8 us (10%)
  between operations  21.9 us (10%)
  local copies, waits for them, and re-layouts  19.7 us (9%)
    unnamed x8, blocking collectives  91 us
    ppermute x8, starting transfers between devices, from_behind(): return lax.ppermute(array, axis, pairs)  22.1 us
    ppermute x8, waiting for transfers between devices, from_behind(): return lax.ppermute(array, axis, pairs)  19.2 us
    unnamed x454, local copies, waits for them, and re-layouts  14.9 us
    unnamed x15, other arithmetic  11.8 us
    ppermute x2, starting transfers between devices, with_halo(): lax.ppermute(lax.slice_in_dim(block, block.shape[dim] - width, None, axis...  4.81 us
  transfers between devices with their start and end apart: 12, of which 6 were waited for; matrix products, arithmetic and copies ran while one was open for 4% of the time, Pallas kernels for 0%

commit v1 on v0

v1 whole, which is shorter than its diff:
```python
import jax
import jax.numpy as jnp
from jax import lax
from jax.experimental import pallas as pl
from jax.experimental.pallas import tpu as pltpu
from jax.sharding import PartitionSpec as P

ITERS = 2
MESH = pl.DeviceIdType.MESH
LINKS = ((0, 1), (1, 0), (1, 1), (1, -1))
ENDS = LINKS + tuple((-i, -j) for i, j in LINKS)
DAMPING = 64.0
LANES = 128
PAD = 8
F32 = jnp.float32


def pieces(step, size):
    inside = (max(0, -step), max(0, step), size - abs(step), 0)
    if step == 0:
        return [inside]
    if step > 0:
        return [inside, (size - step, 0, step, 1)]
    return [inside, (0, size + step, -step, -1)]


def solve(gram, cross):
    g = lambda a, b: gram[min(a, b), max(a, b)]
    low = [[None] * 4 for _ in range(4)]
    raw = [[None] * 4 for _ in range(4)]
    inv = [None] * 4
    for j in range(4):
        for i in range(j, 4):
            v = g(i, j)
            for k in range(j):
                v = v - low[i][k] * raw[j][k]
            raw[i][j] = v
        inv[j] = 1.0 / raw[j][j]
        for i in range(j + 1, 4):
            low[i][j] = raw[i][j] * inv[j]
    out = []
    for c in range(3):
        z = []
        for i in range(4):
            v = cross[c, i]
            for k in range(i):
                v = v - low[i][k] * z[k]
            z.append(v)
        s = [None] * 4
        for i in (3, 2, 1, 0):
            v = z[i] * inv[i]
            for k in range(i + 1, 4):
                v = v - low[k][i] * s[k]
            s[i] = v
        out.extend(s)
    return out


def make_kernel(n_row, n_col, rows, cols):
    halves = cols // 8
    wide = PAD + cols + 8
    last_r, last_c = PAD + cols - 1, PAD + cols

    remote = []
    local = []
    for d, (di, dj) in enumerate(LINKS):
        for sr, tr, nr, dr in pieces(di, rows):
            for sc, tc, nc, dc in pieces(dj, cols):
                entry = (d, pl.ds(sr, nr), pl.ds(sc, nc), pl.ds(tr, nr), pl.ds(tc, nc), dr, dc)
                (local if dr == 0 and dc == 0 else remote).append(entry)
    n_remote = 3 * len(remote)
    n_local = 3 * len(local)

    def kernel(
        here, there, mask, tf, aligned, stats,
        xs, zs, ms, wm, ys, errs, tfv, axl, edge, hrow, sums, msg, got_c, got_r, rec,
        own_sem, loc_sem, tf_sem, pts_send, pts_recv, halo_send, halo_recv,
        c_send, c_recv, r_send, r_recv,
    ):
        r = lax.axis_index("row")
        c = lax.axis_index("col")

        def at(dr, dc):
            return (lax.rem(r + dr + n_row, n_row), lax.rem(c + dc + n_col, n_col))

        barrier = pltpu.get_barrier_semaphore()
        for s in range(1, n_row):
            pl.semaphore_signal(barrier, inc=1, device_id=at(s, 0), device_id_type=MESH)
        for s in range(1, n_col):
            pl.semaphore_signal(barrier, inc=1, device_id=at(0, s), device_id_type=MESH)
        for dr in (-1, 1):
            for dc in (-1, 1):
                pl.semaphore_signal(barrier, inc=1, device_id=at(dr, dc), device_id_type=MESH)

        tf_copy = pltpu.make_async_copy(tf, tfv, tf_sem)
        tf_copy.start()
        own = [
            pltpu.make_async_copy(here, xs.at[pl.ds(0, 4)], own_sem.at[0]),
            pltpu.make_async_copy(there, zs.at[pl.ds(0, 4)], own_sem.at[1]),
            pltpu.make_async_copy(mask, ms.at[pl.ds(0, 4)], own_sem.at[2]),
        ]
        for copy in own:
            copy.start()
        inner = []
        for n, (d, sr, sc, tr, tc, _, _) in enumerate(local):
            inner += [
                pltpu.make_async_copy(
                    there.at[d, :, sr, sc, :], xs.at[4 + d, :, tr, tc, :], loc_sem.at[3 * n]),
                pltpu.make_async_copy(
                    here.at[d, :, sr, sc, :], zs.at[4 + d, :, tr, tc, :], loc_sem.at[3 * n + 1]),
                pltpu.make_async_copy(
                    mask.at[d, sr, sc, :], ms.at[4 + d, tr, tc, :], loc_sem.at[3 * n + 2]),
            ]
        for copy in inner:
            copy.start()

        lane = lax.broadcasted_iota(jnp.int32, (cols, LANES), 1)
        sub = lax.broadcasted_iota(jnp.int32, (cols, LANES), 0)
        eye = lane == sub
        row_lane = lax.broadcasted_iota(jnp.int32, (1, LANES), 1)

        def halo_copies(t):
            def send(n, src, dst, dr, dc):
                return pltpu.make_async_remote_copy(
                    src_ref=src, dst_ref=dst, send_sem=halo_send.at[t, n],
                    recv_sem=halo_recv.at[t, n], device_id=at(dr, dc), device_id_type=MESH)

            a = axl.at[t]
            every = pl.ds(0, 12)
            mid = pl.ds(1, rows)
            first, last = pl.ds(PAD, 1), pl.ds(last_r, 1)
            before, after = pl.ds(PAD - 1, 1), pl.ds(last_c, 1)
            top, bottom = pl.ds(1, 1), pl.ds(rows, 1)
            above, under = pl.ds(0, 1), pl.ds(rows + 1, 1)
            return [
                send(0, edge.at[t, 0], hrow.at[t, 1], -1, 0),
                send(1, edge.at[t, 1], hrow.at[t, 0], 1, 0),
                send(2, a.at[every, mid, first, :], a.at[every, mid, after, :], 0, -1),
                send(3, a.at[every, mid, last, :], a.at[every, mid, before, :], 0, 1),
                send(4, a.at[every, top, first, :], a.at[every, under, after, :], -1, -1),
                send(5, a.at[every, top, last, :], a.at[every, under, before, :], -1, 1),
                send(6, a.at[every, bottom, first, :], a.at[every, above, after, :], 1, -1),
                send(7, a.at[every, bottom, last, :], a.at[every, above, before, :], 1, 1),
            ]

        def publish(t):
            for side, i in ((0, 0), (1, rows - 1)):
                packed = jnp.zeros((cols, LANES), F32)
                for k in range(12):
                    packed = jnp.where(lane == k, axl[t, k, 1 + i, PAD : PAD + cols, :], packed)
                edge[t, side] = packed

        tf_copy.wait()
        for k in range(12):
            for i in range(rows):
                line = tfv[k // 4, k % 4, i : i + 1, :]
                spread = jnp.where(eye[:, :cols], jnp.broadcast_to(line, (cols, cols)), 0.0)
                value = jnp.sum(spread, axis=1, keepdims=True)
                axl[0, k, 1 + i, PAD : PAD + cols, :] = jnp.broadcast_to(value, (cols, LANES))
        publish(0)

        pl.semaphore_wait(barrier, n_row - 1 + n_col - 1 + 4)

        halos = halo_copies(0)
        for copy in halos:
            copy.start()
        outer = []
        for n, (d, sr, sc, tr, tc, dr, dc) in enumerate(remote):
            for m, (src, dst) in enumerate((
                (there.at[d, :, sr, sc, :], xs.at[4 + d, :, tr, tc, :]),
                (here.at[d, :, sr, sc, :], zs.at[4 + d, :, tr, tc, :]),
                (mask.at[d, sr, sc, :], ms.at[4 + d, tr, tc, :]),
            )):
                outer.append(pltpu.make_async_remote_copy(
                    src_ref=src, dst_ref=dst, send_sem=pts_send.at[3 * n + m],
                    recv_sem=pts_recv.at[3 * n + m], device_id=at(dr, dc),
                    device_id_type=MESH))
        for copy in outer:
            copy.start()

        def masks(e):
            di, dj = ENDS[e]
            j = c * cols + sub + dj
            keep_col = (j >= 0) & (j < n_col * cols)
            for i in range(rows):
                row = r * rows + i + di
                keep = keep_col & (row >= 0) & (row < n_row * rows)
                wm[e, i] = jnp.where(keep, ms[e, i].astype(F32), 0.0)

        for copy in own:
            copy.wait()
        for e in range(4):
            masks(e)
        count = jnp.zeros((8, LANES), F32)
        for e in range(4):
            for i in range(rows):
                for h in range(halves):
                    count = count + wm[e, i, 8 * h : 8 * h + 8, :]

        def all_sum(x):
            return jnp.sum(jnp.sum(x, axis=0, keepdims=True), axis=1, keepdims=True)

        def all_max(x):
            return jnp.max(jnp.max(x, axis=0, keepdims=True), axis=1, keepdims=True)

        count = all_sum(count)

        def errors(t, group, carry):
            def body(i, carry):
                top, total = carry
                for h in range(halves):
                    lo = 8 * h
                    own_map = [axl[t, k, 1 + i, PAD + lo : PAD + lo + 8, :] for k in range(12)]
                    for e in group:
                        di, dj = ENDS[e]
                        x = [xs[e, n, i, lo : lo + 8, :] for n in range(3)]
                        z = [zs[e, n, i, lo : lo + 8, :] for n in range(3)]
                        err = None
                        for q in range(3):
                            far = [
                                axl[t, 4 * q + k, 1 + di + i,
                                    PAD + dj + lo : PAD + dj + lo + 8, :]
                                for k in range(4)
                            ]
                            y = far[3] + far[0] * z[0]
                            y = y + far[1] * z[1]
                            y = y + far[2] * z[2]
                            ys[e, q, i, lo : lo + 8, :] = y
                            a = own_map[4 * q + 3] + own_map[4 * q] * x[0]
                            a = a + own_map[4 * q + 1] * x[1]
                            a = a + own_map[4 * q + 2] * x[2]
                            gap = a - y
                            err = gap * gap if err is None else err + gap * gap
                        errs[e, i, lo : lo + 8, :] = err
                        if carry is not None:
                            masked = wm[e, i, lo : lo + 8, :] * err
                            top = jnp.maximum(top, masked)
                            total = total + masked
                return top, total

            return lax.fori_loop(0, rows, body, carry)

        def moments(scale):
            def body(i, _):
                for h in range(halves):
                    lo = 8 * h
                    acc = [None] * 22
                    for e in range(8):
                        w = wm[e, i, lo : lo + 8, :] * (scale / (scale + errs[e, i, lo : lo + 8, :]))
                        x = [xs[e, n, i, lo : lo + 8, :] for n in range(3)]
                        y = [ys[e, n, i, lo : lo + 8, :] for n in range(3)]
                        wx = [w * v for v in x]
                        new = []
                        for a in range(3):
                            for b in range(a, 3):
                                new.append(wx[a] * x[b])
                            new.append(wx[a])
                        new.append(w)
                        for q in range(3):
                            wy = w * y[q]
                            new += [wy * v for v in x]
                            new.append(wy)
                        acc = [n if a is None else a + n for a, n in zip(acc, new)]
                    for n in range(22):
                        total = jnp.sum(acc[n], axis=1, keepdims=True)
                        sums[n, i, lo : lo + 8, :] = jnp.broadcast_to(total, (8, LANES))
                return 0

            lax.fori_loop(0, rows, body, 0)

        pending = []
        for t in range(ITERS):
            for n in (0, 2, 3, 4, 5, 1, 6, 7):
                halos[n].wait_recv()
            for side, row in ((1, rows + 1), (0, 0)):
                block = hrow[t, side]
                for k in range(12):
                    axl[t, k, row, PAD : PAD + cols, :] = jnp.broadcast_to(
                        block[:, k : k + 1], (cols, LANES))
            zero = jnp.zeros((8, LANES), F32)
            top, total = errors(t, range(4), (zero, zero))
            top, total = all_max(top), all_sum(total)
            packed = jnp.where(row_lane < 32, top, jnp.where(row_lane < 64, total, count))

            def combine(block):
                return jnp.where(
                    row_lane < 32, jnp.max(block, axis=0, keepdims=True),
                    jnp.sum(block, axis=0, keepdims=True))

            def share(packed, stage, got, me, size, send_sem, recv_sem, target):
                msg[t, stage] = packed
                got[t, pl.ds(me, 1), :] = packed
                for s in range(1, size):
                    pltpu.make_async_remote_copy(
                        src_ref=msg.at[t, stage], dst_ref=got.at[t, pl.ds(me, 1), :],
                        send_sem=send_sem.at[t], recv_sem=recv_sem.at[t],
                        device_id=target(s), device_id_type=MESH).start()

            def arrived(got, size, sem):
                block = got.at[t, pl.ds(0, size - 1), :]
                pltpu.make_async_copy(block, block, sem.at[t]).wait()

            share(packed, 0, got_c, c, n_col, c_send, c_recv, lambda s: at(0, s))
            arrived(got_c, n_col, c_recv)
            share(combine(got_c[t]), 1, got_r, r, n_row, r_send, r_recv, lambda s: at(s, 0))
            if t == 0:
                for copy in inner:
                    copy.wait()
                for copy in outer:
                    copy.wait_recv()
                for e in range(4, 8):
                    masks(e)
            errors(t, range(4, 8), (zero, zero))
            arrived(got_r, n_row, r_recv)
            packed = combine(got_r[t])
            largest, total, number = packed[:, 0:1], packed[:, 32:33], packed[:, 64:65]
            mean = total / jnp.maximum(number, 1.0)
            scale = 0.25 * largest + 1e-6
            damping = DAMPING * mean + 1.0
            rec[t, 0] = jnp.broadcast_to(largest, (1, LANES))
            rec[t, 1] = jnp.broadcast_to(mean, (1, LANES))
            moments(jnp.broadcast_to(scale, (8, LANES)))
            damp = jnp.broadcast_to(damping, (cols, LANES))
            for i in range(rows):
                old = [axl[t, k, 1 + i, PAD : PAD + cols, :] for k in range(12)]
                gram, n = {}, 0
                for a in range(4):
                    for b in range(a, 4):
                        gram[a, b] = sums[n, i] + damp if a == b else sums[n, i]
                        n += 1
                cross = {}
                for q in range(3):
                    for b in range(4):
                        cross[q, b] = sums[n, i] + damp * old[4 * q + b]
                        n += 1
                new = solve(gram, cross)
                if t + 1 < ITERS:
                    for k in range(12):
                        axl[t + 1, k, 1 + i, PAD : PAD + cols, :] = new[k]
                else:
                    for k in range(12):
                        line = jnp.sum(jnp.where(eye, new[k], 0.0), axis=0, keepdims=True)
                        aligned[k // 4, k % 4, i : i + 1, :] = line[:, :cols]
            pending += halos
            if t + 1 < ITERS:
                publish(t + 1)
                halos = halo_copies(t + 1)
                for copy in halos:
                    copy.start()

        a = lax.broadcasted_iota(jnp.int32, (2, 2), 1)
        b = lax.broadcasted_iota(jnp.int32, (2, 2), 0)
        stats[...] = jnp.where(
            b == 0,
            jnp.where(a == 0, rec[0, 0][:, :2], rec[1, 0][:, :2]),
            jnp.where(a == 0, rec[0, 1][:, :2], rec[1, 1][:, :2]))

        for copy in pending + outer:
            copy.wait_send()
        for t in range(ITERS):
            for got, size, sem in ((got_c, n_col, c_send), (got_r, n_row, r_send)):
                block = got.at[t, pl.ds(0, size - 1), :]
                pltpu.make_async_copy(block, block, sem.at[t]).wait()

    dma = pltpu.SemaphoreType.DMA
    vm = pltpu.VMEM
    scratch = [
        vm((8, 3, rows, cols, LANES), F32),
        vm((8, 3, rows, cols, LANES), F32),
        vm((8, rows, cols, LANES), jnp.int32),
        vm((8, rows, cols, LANES), F32),
        vm((8, 3, rows, cols, LANES), F32),
        vm((8, rows, cols, LANES), F32),
        vm((3, 4, rows, cols), F32),
        vm((ITERS, 12, rows + 2, wide, LANES), F32),
        vm((ITERS, 2, cols, LANES), F32),
        vm((ITERS, 2, cols, LANES), F32),
        vm((22, rows, cols, LANES), F32),
        vm((ITERS, 2, 1, LANES), F32),
        vm((ITERS, n_col, LANES), F32),
        vm((ITERS, n_row, LANES), F32),
        vm((ITERS, 2, 1, LANES), F32),
        dma((3,)), dma((n_local,)), dma(()),
        dma((n_remote,)), dma((n_remote,)),
        dma((ITERS, 8)), dma((ITERS, 8)),
        dma((ITERS,)), dma((ITERS,)), dma((ITERS,)), dma((ITERS,)),
    ]
    return kernel, scratch


def solution(mesh):
    n_row, n_col = mesh.shape["row"], mesh.shape["col"]

    def on_device(points_here, points_there, outlier_mask, transforms):
        rows, cols = transforms.shape[2:]
        kernel, scratch = make_kernel(n_row, n_col, rows, cols)
        hbm = pl.BlockSpec(memory_space=pl.ANY)
        return pl.pallas_call(
            kernel,
            out_shape=(
                jax.ShapeDtypeStruct(transforms.shape, F32),
                jax.ShapeDtypeStruct((2, ITERS), F32),
            ),
            in_specs=[hbm] * 4,
            out_specs=(pl.BlockSpec(memory_space=pltpu.VMEM),) * 2,
            scratch_shapes=scratch,
            compiler_params=pltpu.CompilerParams(
                collective_id=0, has_side_effects=True, vmem_limit_bytes=48 << 20),
        )(points_here, points_there, outlier_mask, transforms)

    placed = (
        P(None, None, "row", "col", None),
        P(None, None, "row", "col", None),
        P(None, "row", "col", None),
        P(None, None, "row", "col"),
    )
    return jax.shard_map(
        on_device, mesh=mesh, in_specs=placed,
        out_specs=(P(None, None, "row", "col"), P()), check_vma=False)
```

time: 218 us -> 54.4 us (0.25)
  the two profiles are of different devices: /device:TPU:66 before, /device:TPU:1 now
where the time goes in v1:
time: 54.4 us; the launch traced here: 54.1 us
  Pallas kernels  48.6 us (89%)
  local copies, waits for them, and re-layouts  4.8 us (9%)
  between operations  0.65 us (1%)
    pallas_call x1, Pallas kernels, on_device(): pl.pallas_call(kernel, out_shape=(jax.ShapeDtypeStruct(transforms.shape,...  48.6 us
    unnamed x10, local copies, waits for them, and re-layouts  4.8 us

profile of v1, /device:TPU:1, one launch (start us, length us, event | category | flops | bytes accessed | tf_op | source)
XLA Modules:
  0.0 54.1 jit_solution(2742883121152535079)
XLA Ops:
  0.6 0.0 copy-start
  0.6 1.0 %copy-done = f32[4,3,4,16,128]{4,3,2,1,0:T(8,128)S(1)} copy-done((f32[4,3,4,16,128]{4,3,2,1,0:T(8,128)S(1)}, f32[4,3,4,16,128]{4,3,2,1,0:T(8,128)}, u32[]{:S(2)}) %copy-start) | copy-done | bytes 393240
  1.6 0.0 copy-start.1
  1.6 1.0 %copy-done.1 = f32[4,3,4,16,128]{4,3,2,1,0:T(8,128)S(1)} copy-done((f32[4,3,4,16,128]{4,3,2,1,0:T(8,128)S(1)}, f32[4,3,4,16,128]{4,3,2,1,0:T(8,128)}, u32[]{:S(2)}) %copy-start.1) | copy-done | bytes 393240
  2.6 0.0 copy-start.2
  2.6 0.9 %copy-done.2 = s32[4,4,16,128]{3,2,1,0:T(8,128)S(1)} copy-done((s32[4,4,16,128]{3,2,1,0:T(8,128)S(1)}, s32[4,4,16,128]{3,2,1,0:T(8,128)}, u32[]{:S(2)}) %copy-start.2) | copy-done | bytes 131096
  3.5 0.0 copy-start.3
  3.5 0.7 %copy-done.3 = f32[3,4,4,16]{3,2,1,0:T(4,128)S(1)} copy-done((f32[3,4,4,16]{3,2,1,0:T(4,128)S(1)}, f32[3,4,4,16]{3,2,1,0:T(4,128)}, u32[]{:S(2)}) %copy-start.3) | copy-done | bytes 3096
  4.3 48.6 %shard_map.59 = (f32[3,4,4,16]{3,2,1,0:T(4,128)S(1)}, f32[2,2]{1,0:T(2,128)S(1)}) custom-call(f32[4,3,4,16,128]{4,3,2,1,0:T(8,128)S(1)} %copy-done, f32[4,3,4,16,128]{4,3,2,1,0:T(8,128)S(1)} %copy-done.1, s32[4,4,16,128]{3,2,1,0:T(8,128)S(1)} %copy-done.2, f32[3,4,4,16]{3,2,1,0:T(4,128)S(1)} %copy-done.3), custom_call_target="tpu_custom_call" | custom-call | tf_op jit(solution)/shard_map/pallas_call | solution.py:398
  52.9 0.6 %copy.8 = f32[3,4,4,16]{3,2,1,0:T(4,128)} copy(f32[3,4,4,16]{3,2,1,0:T(4,128)S(1)} %get-tuple-element.4) | data formatting | bytes 6144
  53.5 0.6 %copy.9 = f32[2,2]{1,0:T(2,128)} copy(f32[2,2]{1,0:T(2,128)S(1)} %get-tuple-element.5) | data formatting | bytes 32
Async XLA Ops:
  0.6 1.0 %copy-start = (f32[4,3,4,16,128]{4,3,2,1,0:T(8,128)S(1)}, f32[4,3,4,16,128]{4,3,2,1,0:T(8,128)}, u32[]{:S(2)}) copy-start(f32[4,3,4,16,128]{4,3,2,1,0:T(8,128)} %here.1) | copy-start | bytes 1179652
  1.6 1.0 %copy-start.1 = (f32[4,3,4,16,128]{4,3,2,1,0:T(8,128)S(1)}, f32[4,3,4,16,128]{4,3,2,1,0:T(8,128)}, u32[]{:S(2)}) copy-start(f32[4,3,4,16,128]{4,3,2,1,0:T(8,128)} %there.1) | copy-start | bytes 1179652
  2.6 0.9 %copy-start.2 = (s32[4,4,16,128]{3,2,1,0:T(8,128)S(1)}, s32[4,4,16,128]{3,2,1,0:T(8,128)}, u32[]{:S(2)}) copy-start(s32[4,4,16,128]{3,2,1,0:T(8,128)} %mask.1) | copy-start | bytes 393220
  3.5 0.7 %copy-start.3 = (f32[3,4,4,16]{3,2,1,0:T(4,128)S(1)}, f32[3,4,4,16]{3,2,1,0:T(4,128)}, u32[]{:S(2)}) copy-start(f32[3,4,4,16]{3,2,1,0:T(4,128)} %tf.1) | copy-start | bytes 9220

commit v2 on v1

v2 whole, which is shorter than its diff:
```python
import jax
import jax.numpy as jnp
from jax import lax
from jax.experimental import pallas as pl
from jax.experimental.pallas import tpu as pltpu
from jax.sharding import PartitionSpec as P

ITERS = 2
MESH = pl.DeviceIdType.MESH
LINKS = ((0, 1), (1, 0), (1, 1), (1, -1))
DAMPING = 64.0
LANES = 128
RING = 2
WIDE = 32
COL0 = 3
NX, NY = 4, 8
F32 = jnp.float32


def solve(gram, cross):
    g = lambda a, b: gram[min(a, b), max(a, b)]
    low = [[None] * 4 for _ in range(4)]
    raw = [[None] * 4 for _ in range(4)]
    inv = [None] * 4
    for j in range(4):
        for i in range(j, 4):
            v = g(i, j)
            for k in range(j):
                v = v - low[i][k] * raw[j][k]
            raw[i][j] = v
        inv[j] = 1.0 / raw[j][j]
        for i in range(j + 1, 4):
            low[i][j] = raw[i][j] * inv[j]
    out = []
    for c in range(3):
        z = []
        for i in range(4):
            v = cross[c, i]
            for k in range(i):
                v = v - low[i][k] * z[k]
            z.append(v)
        s = [None] * 4
        for i in (3, 2, 1, 0):
            v = z[i] * inv[i]
            for k in range(i + 1, 4):
                v = v - low[k][i] * s[k]
            s[i] = v
        out.extend(s)
    return out


def make_kernel(n_row, n_col, rows, cols):
    around = [(a, b) for a in (-1, 0, 1) for b in (-1, 0, 1) if (a, b) != (0, 0)]
    span = rows + 2 * RING - 1

    def kernel(
        here, there, mask, tf, aligned, stats,
        xs, zs, ms, wm, wt, hm, tm, errs, tfv, axl, sums, msg, got_c, got_r, rec,
        own_sem, tf_sem, pts_send, pts_recv, tf_send, tf_recv,
        c_send, c_recv, r_send, r_recv, known,
    ):
        r = lax.axis_index("row")
        c = lax.axis_index("col")
        x0, y0 = r // NY, lax.rem(r, NY)
        up, down, left, right = r > 0, r < n_row - 1, c > 0, c < n_col - 1
        side = {(-1, 0): up, (1, 0): down, (0, -1): left, (0, 1): right}

        def exists(dr, dc):
            if dr and dc:
                return side[dr, 0] & side[0, dc]
            return side[dr, dc]

        def at_col(s):
            return (r, lax.rem(c + s + n_col, n_col))

        def at_xy(dx, dy):
            return (lax.rem(x0 + dx + NX, NX) * NY + lax.rem(y0 + dy + NY, NY), c)

        def signal(sem, device):
            pl.semaphore_signal(sem, inc=1, device_id=device, device_id_type=MESH)

        one = lambda flag: flag.astype(jnp.int32)
        barrier = pltpu.get_barrier_semaphore()
        steps_xy = ((0, 1), (0, -1), (1, 0), (-1, 0))
        for d in steps_xy:
            signal(barrier, at_xy(*d))
        for s in (1, -1, 2, -2):
            signal(barrier, at_col(s))
        greeted = 8
        cross_up, cross_down = up & (y0 == 0), down & (y0 == NY - 1)
        for dr, dc, flag in (
            (-1, 0, cross_up), (1, 0, cross_down),
            (-1, -1, exists(-1, -1)), (-1, 1, exists(-1, 1)),
            (1, -1, exists(1, -1)), (1, 1, exists(1, 1)),
        ):
            greeted = greeted + one(flag)

            @pl.when(flag)
            def _():
                signal(barrier, (r + dr, c + dc))

        middle_r, middle_c = pl.ds(RING, rows), pl.ds(COL0, cols)
        own = [
            pltpu.make_async_copy(tf, tfv.at[4], tf_sem),
            pltpu.make_async_copy(mask, ms.at[:, middle_r, middle_c, :], own_sem.at[2]),
            pltpu.make_async_copy(here, xs.at[:, :, middle_r, middle_c, :], own_sem.at[0]),
            pltpu.make_async_copy(there, zs.at[:, :, middle_r, middle_c, :], own_sem.at[1]),
        ]
        for copy in own:
            copy.start()

        for dr, dc in around:
            @pl.when(jnp.logical_not(exists(dr, dc)))
            def _():
                tfv[(dr + 1) * 3 + dc + 1] = jnp.zeros((3, 4, rows, cols), F32)

        def blank(row_part, col_part):
            for buf in (xs, zs):
                shape = (4, 3, row_part.size, col_part.size, LANES)
                buf[:, :, row_part, col_part, :] = jnp.zeros(shape, F32)

        for flag, row_part, col_part in (
            (up, pl.ds(0, RING), pl.ds(0, WIDE)),
            (down, pl.ds(RING + rows, 1), pl.ds(0, WIDE)),
            (left, pl.ds(0, span), pl.ds(0, COL0)),
            (right, pl.ds(0, span), pl.ds(COL0 + cols, RING)),
        ):
            @pl.when(jnp.logical_not(flag))
            def _():
                blank(row_part, col_part)

        lane16 = lax.broadcasted_iota(jnp.int32, (8, cols), 1)
        sub8 = lax.broadcasted_iota(jnp.int32, (8, cols), 0)
        row_lane = lax.broadcasted_iota(jnp.int32, (1, LANES), 1)

        pl.semaphore_wait(barrier, greeted)

        def tf_copy(n, dr, dc):
            return pltpu.make_async_remote_copy(
                src_ref=tf, dst_ref=tfv.at[(1 - dr) * 3 + 1 - dc], send_sem=tf_send.at[n],
                recv_sem=tf_recv.at[n], device_id=(r + dr, c + dc), device_id_type=MESH)

        def tf_arrived(dr, dc):
            n = around.index((-dr, -dc))

            @pl.when(exists(dr, dc))
            def _():
                tf_copy(n, -dr, -dc).wait_recv()

        for dr, dc in ((1, 1), (1, -1), (-1, 1), (-1, -1), (1, 0), (-1, 0), (0, 1), (0, -1)):
            @pl.when(exists(dr, dc))
            def _():
                tf_copy(around.index((dr, dc)), dr, dc).start()

        for d in steps_xy:
            signal(known.at[0], at_xy(*d))
        signal(known.at[0], at_col(2))
        signal(known.at[0], at_col(-2))

        part_r = {1: (rows - RING, 0, RING), 0: (0, RING, rows), -1: (0, RING + rows, 1)}
        part_c = {
            1: (cols - RING, COL0 - RING, RING), 0: (0, COL0, cols), -1: (0, COL0 + cols, RING)}

        def outer(dr, dc):
            n = around.index((dr, dc))
            sr, tr, nr = part_r[dr]
            sc, tc, nc = part_c[dc]
            src = (pl.ds(sr, nr), pl.ds(sc, nc), slice(None))
            dst = (pl.ds(tr, nr), pl.ds(tc, nc), slice(None))
            every = (slice(None),)
            return [
                pltpu.make_async_remote_copy(
                    src_ref=a.at[lead + src], dst_ref=b.at[lead + dst],
                    send_sem=pts_send.at[n, m], recv_sem=pts_recv.at[n, m],
                    device_id=(r + dr, c + dc), device_id_type=MESH)
                for m, (a, b, lead) in enumerate(
                    ((here, xs, every * 2), (there, zs, every * 2), (mask, ms, every)))
            ]

        for dr, dc in around:
            @pl.when(exists(dr, dc))
            def _():
                for copy in outer(dr, dc):
                    copy.start()

        def masks(d, i, lo, size):
            di, dj = LINKS[d]
            sub = lax.broadcasted_iota(jnp.int32, (size, LANES), 0)
            j = c * cols + sub + (lo - COL0)
            k = j + dj
            row = r * rows + i
            keep_row = (row >= 0) & (row + di < n_row * rows)
            keep = (j >= 0) & (j < n_col * cols) & (k >= 0) & (k < n_col * cols) & keep_row
            wm[d, RING + i, lo : lo + size, :] = jnp.where(
                keep, ms[d, RING + i, lo : lo + size, :].astype(F32), 0.0)

        own[1].wait()
        count = jnp.zeros((cols, LANES), F32)
        for d in range(4):
            for i in range(rows):
                masks(d, i, COL0, cols)
                count = count + wm[d, RING + i, COL0 : COL0 + cols, :]

        def all_sum(x):
            return jnp.sum(jnp.sum(x, axis=0, keepdims=True), axis=1, keepdims=True)

        def all_max(x):
            return jnp.max(jnp.max(x, axis=0, keepdims=True), axis=1, keepdims=True)

        count = all_sum(count)

        pl.semaphore_wait(known.at[0], 6)
        for device in (at_xy(0, 2), at_xy(0, -2), at_xy(2, 0), at_col(4), at_col(-4)):
            signal(known.at[1], device)

        own_lane = lane16 - sub8
        picks = (
            ((4, own_lane == -COL0), (3, own_lane == cols - COL0)),
            ((4, own_lane == 8 - COL0),),
            ((4, own_lane == 16 - COL0), (5, own_lane == 16 - COL0 - cols)),
        )

        def expand(i):
            base = 3 if 0 <= i < rows else (0 if i < 0 else 6)
            row = i % rows
            for k in range(12):
                for b, pick in enumerate(picks):
                    total = None
                    for slot, chosen in pick:
                        line = tfv[base + slot - 3, k // 4, k % 4, row : row + 1, :]
                        part = jnp.where(chosen, jnp.broadcast_to(line, (8, cols)), 0.0)
                        total = part if total is None else total + part
                    value = jnp.sum(total, axis=1, keepdims=True)
                    axl[0, k, RING + i, 8 * b : 8 * b + 8, :] = jnp.broadcast_to(value, (8, LANES))

        def errors(t, first, last, starts, carry=None):
            def body(i, carry):
                for lo in starts:
                    own_map = [axl[t, k, i, lo : lo + 8, :] for k in range(12)]
                    for d in range(4):
                        di, dj = LINKS[d]
                        x = [xs[d, n, i, lo : lo + 8, :] for n in range(3)]
                        z = [zs[d, n, i, lo : lo + 8, :] for n in range(3)]
                        err = None
                        for q in range(3):
                            far = [
                                axl[t, 4 * q + k, i + di, lo + dj : lo + dj + 8, :]
                                for k in range(4)
                            ]
                            y = far[3] + far[0] * z[0]
                            y = y + far[1] * z[1]
                            y = y + far[2] * z[2]
                            tm[d, q, i, lo : lo + 8, :] = y
                            a = own_map[4 * q + 3] + own_map[4 * q] * x[0]
                            a = a + own_map[4 * q + 1] * x[1]
                            a = a + own_map[4 * q + 2] * x[2]
                            hm[d, q, i, lo : lo + 8, :] = a
                            gap = a - y
                            err = gap * gap if err is None else err + gap * gap
                        errs[d, i, lo : lo + 8, :] = err
                        if carry is not None:
                            masked = wm[d, i, lo : lo + 8, :] * err
                            carry = (jnp.maximum(carry[0], masked), carry[1] + masked)
                return carry

            if carry is None:
                lax.fori_loop(first, last, lambda i, _: body(i, None) or 0, 0)
                return None
            return lax.fori_loop(first, last, body, carry)

        def weights(first, last, starts, scale):
            def body(i, _):
                for lo in starts:
                    for d in range(4):
                        at = (d, i, slice(lo, lo + 8))
                        wt[at] = wm[at] * (scale / (scale + errs[at]))
                return 0

            lax.fori_loop(first, last, body, 0)

        def moments(first, last, starts):
            def body(i, _):
                for lo in starts:
                    acc = [None] * 22
                    for e in range(8):
                        d = e % 4
                        di, dj = LINKS[d] if e >= 4 else (0, 0)
                        p, q = i - di, lo - dj
                        w = wt[d, p, q : q + 8, :]
                        mine, other = (xs, tm) if e < 4 else (zs, hm)
                        x = [mine[d, n, p, q : q + 8, :] for n in range(3)]
                        y = [other[d, n, p, q : q + 8, :] for n in range(3)]
                        wx = [w * v for v in x]
                        new = []
                        for a in range(3):
                            for b in range(a, 3):
                                new.append(wx[a] * x[b])
                            new.append(wx[a])
                        new.append(w)
                        for n in range(3):
                            wy = w * y[n]
                            new += [wy * v for v in x]
                            new.append(wy)
                        acc = [n if a is None else a + n for a, n in zip(acc, new)]
                    for n in range(22):
                        total = jnp.sum(acc[n], axis=1, keepdims=True)
                        sums[n, i, lo : lo + 8, :] = jnp.broadcast_to(total, (8, LANES))
                return 0

            lax.fori_loop(first, last, body, 0)

        own[0].wait()
        for spot in ((0, 1), (0, -1), (1, 0), (1, 1), (1, -1)):
            tf_arrived(*spot)
        for i in range(rows + 1):
            expand(i)
        own[2].wait()
        own[3].wait()

        def combine(block):
            return jnp.where(
                row_lane < 32, jnp.max(block, axis=0, keepdims=True),
                jnp.sum(block, axis=0, keepdims=True))

        def share(t, packed, stage, got, me, send_sem, recv_sem, targets):
            msg[t, stage] = packed
            got[t, pl.ds(me, 1), :] = packed
            for device in targets:
                pltpu.make_async_remote_copy(
                    src_ref=msg.at[t, stage], dst_ref=got.at[t, pl.ds(me, 1), :],
                    send_sem=send_sem.at[t], recv_sem=recv_sem.at[t],
                    device_id=device, device_id_type=MESH).start()

        def arrived(t, got, size, sem):
            block = got.at[t, pl.ds(0, size - 1), :]
            pltpu.make_async_copy(block, block, sem.at[t]).wait()

        col_targets = [at_col(s) for s in sorted(range(1, n_col), key=lambda s: -min(s, n_col - s))]
        plane = [(a, b) for a in range(NX) for b in range(NY) if a or b]
        plane.sort(key=lambda p: -(min(p[0], NX - p[0]) + min(p[1], NY - p[1])))
        row_targets = [at_xy(*p) for p in plane]

        own_starts = tuple(range(COL0, COL0 + cols, 8))
        for t in range(ITERS):
            zero = jnp.zeros((8, LANES), F32)
            top, total = errors(t, RING, RING + rows, own_starts, (zero, zero))
            top, total = all_max(top), all_sum(total)
            packed = jnp.where(row_lane < 32, top, jnp.where(row_lane < 64, total, count))
            if t == 0:
                pl.semaphore_wait(known.at[1], 5)
                signal(known.at[2], at_xy(0, 4))
            share(t, packed, 0, got_c, c, c_send, c_recv, col_targets)
            if t == 0:
                for spot in ((-1, 0), (-1, -1), (-1, 1)):
                    tf_arrived(*spot)
                for i in (-2, -1, rows + 1):
                    expand(i)
                pl.semaphore_wait(known.at[2], 1)
            else:
                errors(t, RING - 1, RING, (2, 10, 18))
                errors(t, RING, RING + rows, (2, 18))
            arrived(t, got_c, n_col, c_recv)
            share(t, combine(got_c[t]), 1, got_r, r, r_send, r_recv, row_targets)
            if t == 0:
                for dr, dc in around:
                    @pl.when(exists(dr, dc))
                    def _():
                        for copy in outer(-dr, -dc):
                            copy.wait_recv()
                for d in range(4):
                    for i in range(-RING, rows + 1):
                        if 0 <= i < rows:
                            masks(d, i, 0, 8)
                            masks(d, i, 16, 8)
                        else:
                            masks(d, i, 0, 24)
                errors(t, 0, RING, (1, 9, 17))
                errors(t, RING + rows, RING + rows + 1, (1, 9, 17))
                errors(t, RING, RING + rows, (1, 17))
            arrived(t, got_r, n_row, r_recv)
            packed = combine(got_r[t])
            largest, total, number = packed[:, 0:1], packed[:, 32:33], packed[:, 64:65]
            mean = total / jnp.maximum(number, 1.0)
            scale = jnp.broadcast_to(0.25 * largest + 1e-6, (8, LANES))
            damping = DAMPING * mean + 1.0
            rec[t, 0] = jnp.broadcast_to(largest, (1, LANES))
            rec[t, 1] = jnp.broadcast_to(mean, (1, LANES))
            if t == 0:
                weights(0, span, (1, 9, 17), scale)
                first, last, lo, size = RING - 1, RING + rows + 1, COL0 - 1, 24
            else:
                weights(RING - 1, RING + rows, (2, 10, 18), scale)
                first, last, lo, size = RING, RING + rows, COL0, cols
            moments(first, last, range(lo, lo + size, 8))
            damp = jnp.broadcast_to(damping, (size, LANES))
            for i in range(first, last):
                old = [axl[t, k, i, lo : lo + size, :] for k in range(12)]
                gram, n = {}, 0
                for a in range(4):
                    for b in range(a, 4):
                        part = sums[n, i, lo : lo + size, :]
                        gram[a, b] = part + damp if a == b else part
                        n += 1
                cross = {}
                for q in range(3):
                    for b in range(4):
                        cross[q, b] = sums[n, i, lo : lo + size, :] + damp * old[4 * q + b]
                        n += 1
                new = solve(gram, cross)
                if t + 1 < ITERS:
                    for k in range(12):
                        axl[t + 1, k, i, lo : lo + size, :] = new[k]
                else:
                    lane = lax.broadcasted_iota(jnp.int32, (size, LANES), 1)
                    sub = lax.broadcasted_iota(jnp.int32, (size, LANES), 0)
                    for k in range(12):
                        line = jnp.sum(jnp.where(lane == sub, new[k], 0.0), axis=0, keepdims=True)
                        aligned[k // 4, k % 4, i - first : i - first + 1, :] = line[:, :cols]

        a = lax.broadcasted_iota(jnp.int32, (2, 2), 1)
        b = lax.broadcasted_iota(jnp.int32, (2, 2), 0)
        stats[...] = jnp.where(
            b == 0,
            jnp.where(a == 0, rec[0, 0][:, :2], rec[1, 0][:, :2]),
            jnp.where(a == 0, rec[0, 1][:, :2], rec[1, 1][:, :2]))

        for dr, dc in around:
            @pl.when(exists(dr, dc))
            def _():
                tf_copy(around.index((dr, dc)), dr, dc).wait_send()
                for copy in outer(dr, dc):
                    copy.wait_send()
        for t in range(ITERS):
            arrived(t, got_c, n_col, c_send)
            arrived(t, got_r, n_row, r_send)

    dma = pltpu.SemaphoreType.DMA
    vm = pltpu.VMEM
    grid = (span, WIDE, LANES)
    scratch = [
        vm((4, 3) + grid, F32),
        vm((4, 3) + grid, F32),
        vm((4,) + grid, jnp.int32),
        vm((4,) + grid, F32),
        vm((4,) + grid, F32),
        vm((4, 3) + grid, F32),
        vm((4, 3) + grid, F32),
        vm((4,) + grid, F32),
        vm((9, 3, 4, rows, cols), F32),
        vm((ITERS, 12, rows + 2 * RING, WIDE, LANES), F32),
        vm((22,) + grid, F32),
        vm((ITERS, 2, 1, LANES), F32),
        vm((ITERS, n_col, LANES), F32),
        vm((ITERS, n_row, LANES), F32),
        vm((ITERS, 2, 1, LANES), F32),
        dma((3,)), dma(()),
        dma((8, 3)), dma((8, 3)),
        dma((8,)), dma((8,)),
        dma((ITERS,)), dma((ITERS,)), dma((ITERS,)), dma((ITERS,)),
        pltpu.SemaphoreType.REGULAR((3,)),
    ]
    return kernel, scratch


def solution(mesh):
    n_row, n_col = mesh.shape["row"], mesh.shape["col"]

    def on_device(points_here, points_there, outlier_mask, transforms):
        rows, cols = transforms.shape[2:]
        kernel, scratch = make_kernel(n_row, n_col, rows, cols)
        hbm = pl.BlockSpec(memory_space=pltpu.HBM)
        return pl.pallas_call(
            kernel,
            out_shape=(
                jax.ShapeDtypeStruct(transforms.shape, F32),
                jax.ShapeDtypeStruct((2, ITERS), F32),
            ),
            in_specs=[hbm] * 4,
            out_specs=(pl.BlockSpec(memory_space=pltpu.VMEM),) * 2,
            scratch_shapes=scratch,
            compiler_params=pltpu.CompilerParams(collective_id=0, has_side_effects=True),
        )(points_here, points_there, outlier_mask, transforms)

    placed = (
        P(None, None, "row", "col", None),
        P(None, None, "row", "col", None),
        P(None, "row", "col", None),
        P(None, None, "row", "col"),
    )
    return jax.shard_map(
        on_device, mesh=mesh, in_specs=placed,
        out_specs=(P(None, None, "row", "col"), P()), check_vma=False)
```

time: 54.4 us -> 48.8 us (0.90)
  local copies, waits for them, and re-layouts: 4.8 us -> 1.91 us
  Pallas kernels: 48.6 us -> 46 us
    unnamed x10 -> x4, local copies, waits for them, and re-layouts: 4.8 us -> 1.91 us
    pallas_call x1, Pallas kernels: 48.6 us -> 46 us  [on_device(): pl.pallas_call(kernel, out_shape=(jax.ShapeDtypeStruct(transforms.shape,...]
where the time goes in v2:
time: 48.8 us; the launch traced here: 48.6 us
  Pallas kernels  46 us (94%)
  local copies, waits for them, and re-layouts  1.91 us (4%)
  between operations  0.65 us (1%)
    pallas_call x1, Pallas kernels, on_device(): pl.pallas_call(kernel, out_shape=(jax.ShapeDtypeStruct(transforms.shape,...  46 us
    unnamed x4, local copies, waits for them, and re-layouts  1.91 us

profile of v2, /device:TPU:1, one launch (start us, length us, event | category | flops | bytes accessed | tf_op | source)
XLA Modules:
  0.0 48.6 jit_solution(5320935038757974685)
XLA Ops:
  0.6 46.0 %shard_map.59 = (f32[3,4,4,16]{3,2,1,0:T(4,128)}, f32[2,2]{1,0:T(2,128)}) custom-call(f32[4,3,4,16,128]{4,3,2,1,0:T(8,128)} %here.1, f32[4,3,4,16,128]{4,3,2,1,0:T(8,128)} %there.1, s32[4,4,16,128]{3,2,1,0:T(8,128)} %mask.1, f32[3,4,4,16]{3,2,1,0:T(4,128)} %tf.1), custom_call_target="tpu_custom_call" | custom-call | tf_op jit(solution)/shard_map/pallas_call | solution.py:472
  46.7 0.0 copy-start
  46.7 1.3 %copy.8 = f32[3,4,4,16]{3,2,1,0:T(4,128)} copy(f32[3,4,4,16]{3,2,1,0:T(4,128)} %get-tuple-element.4) | data formatting | bytes 6144
  48.0 0.0 copy-done
  48.0 0.6 %copy.9 = f32[2,2]{1,0:T(2,128)} copy(f32[2,2]{1,0:T(2,128)S(1)} %copy-done) | data formatting | bytes 32
Async XLA Ops:
  46.7 1.4 %copy-start = (f32[2,2]{1,0:T(2,128)S(1)}, f32[2,2]{1,0:T(2,128)}, u32[]{:S(2)}) copy-start(f32[2,2]{1,0:T(2,128)} %get-tuple-element.5) | copy-start | bytes 52

commit v3 on v2

--- a/solution.py
+++ b/solution.py
@@ -57,7 +57,7 @@
         here, there, mask, tf, aligned, stats,
         xs, zs, ms, wm, wt, hm, tm, errs, tfv, axl, sums, msg, got_c, got_r, rec,
         own_sem, tf_sem, pts_send, pts_recv, tf_send, tf_recv,
-        c_send, c_recv, r_send, r_recv, known,
+        c_send, c_recv, r_send, r_recv, edge_send, edge_recv, known,
     ):
         r = lax.axis_index("row")
         c = lax.axis_index("col")
@@ -109,6 +109,26 @@
         for copy in own:
             copy.start()
 
+        edges = (
+            (1, 0, pl.ds(RING + rows - 1, 1), pl.ds(COL0, cols), pl.ds(RING - 1, 1), pl.ds(COL0, cols)),
+            (1, 1, pl.ds(RING + rows - 1, 1), pl.ds(COL0 + cols - 1, 1),
+             pl.ds(RING - 1, 1), pl.ds(COL0 - 1, 1)),
+            (1, -1, pl.ds(RING + rows - 1, 1), pl.ds(COL0, 1), pl.ds(RING - 1, 1), pl.ds(COL0 + cols, 1)),
+        )
+
+        def edge_copy(n, back=1):
+            dr, dc, sr, sc, tr, tc = edges[n]
+            every = (pl.ds(0, 12),)
+            return pltpu.make_async_remote_copy(
+                src_ref=axl.at[(1,) + every + (sr, sc)], dst_ref=axl.at[(1,) + every + (tr, tc)],
+                send_sem=edge_send.at[n], recv_sem=edge_recv.at[n],
+                device_id=(r + dr * back, c + dc * back), device_id_type=MESH)
+
+        for dr, dc, sr, sc, tr, tc in edges:
+            @pl.when(jnp.logical_not(exists(-dr, -dc)))
+            def _():
+                axl[1, :, tr, tc, :] = jnp.zeros((12, tr.size, tc.size, LANES), F32)
+
         for dr, dc in around:
             @pl.when(jnp.logical_not(exists(dr, dc)))
             def _():
@@ -157,7 +177,7 @@
         signal(known.at[0], at_col(2))
         signal(known.at[0], at_col(-2))
 
-        part_r = {1: (rows - RING, 0, RING), 0: (0, RING, rows), -1: (0, RING + rows, 1)}
+        part_r = {1: (rows - 1, RING - 1, 1), 0: (0, RING, rows), -1: (0, RING + rows, 1)}
         part_c = {
             1: (cols - RING, COL0 - RING, RING), 0: (0, COL0, cols), -1: (0, COL0 + cols, RING)}
 
@@ -167,6 +187,7 @@
             sc, tc, nc = part_c[dc]
             src = (pl.ds(sr, nr), pl.ds(sc, nc), slice(None))
             dst = (pl.ds(tr, nr), pl.ds(tc, nc), slice(None))
+            links = (pl.ds(1, 3) if dr > 0 else pl.ds(0, 4),)
             every = (slice(None),)
             return [
                 pltpu.make_async_remote_copy(
@@ -174,7 +195,7 @@
                     send_sem=pts_send.at[n, m], recv_sem=pts_recv.at[n, m],
                     device_id=(r + dr, c + dc), device_id_type=MESH)
                 for m, (a, b, lead) in enumerate(
-                    ((here, xs, every * 2), (there, zs, every * 2), (mask, ms, every)))
+                    ((here, xs, links + every), (there, zs, links + every), (mask, ms, links)))
             ]
 
         for dr, dc in around:
@@ -353,10 +374,14 @@
             if t == 0:
                 for spot in ((-1, 0), (-1, -1), (-1, 1)):
                     tf_arrived(*spot)
-                for i in (-2, -1, rows + 1):
+                for i in (-1, rows + 1):
                     expand(i)
                 pl.semaphore_wait(known.at[2], 1)
             else:
+                for n, (dr, dc, *_) in enumerate(edges):
+                    @pl.when(exists(-dr, -dc))
+                    def _():
+                        edge_copy(n, -1).wait_recv()
                 errors(t, RING - 1, RING, (2, 10, 18))
                 errors(t, RING, RING + rows, (2, 18))
             arrived(t, got_c, n_col, c_recv)
@@ -368,13 +393,13 @@
                         for copy in outer(-dr, -dc):
                             copy.wait_recv()
                 for d in range(4):
-                    for i in range(-RING, rows + 1):
+                    for i in range(-1, rows + 1):
                         if 0 <= i < rows:
                             masks(d, i, 0, 8)
                             masks(d, i, 16, 8)
                         else:
                             masks(d, i, 0, 24)
-                errors(t, 0, RING, (1, 9, 17))
+                errors(t, RING - 1, RING, (1, 9, 17))
                 errors(t, RING + rows, RING + rows + 1, (1, 9, 17))
                 errors(t, RING, RING + rows, (1, 17))
             arrived(t, got_r, n_row, r_recv)
@@ -386,14 +411,15 @@
             rec[t, 0] = jnp.broadcast_to(largest, (1, LANES))
             rec[t, 1] = jnp.broadcast_to(mean, (1, LANES))
             if t == 0:
-                weights(0, span, (1, 9, 17), scale)
-                first, last, lo, size = RING - 1, RING + rows + 1, COL0 - 1, 24
+                weights(RING - 1, span, (1, 9, 17), scale)
+                blocks = [(RING, span, COL0 - 1, 24)]
             else:
                 weights(RING - 1, RING + rows, (2, 10, 18), scale)
-                first, last, lo, size = RING, RING + rows, COL0, cols
-            moments(first, last, range(lo, lo + size, 8))
-            damp = jnp.broadcast_to(damping, (size, LANES))
-            for i in range(first, last):
+                blocks = [(RING, RING + rows, COL0, cols)]
+            for first, last, lo, size in blocks:
+                moments(first, last, range(lo, lo + size, 8))
+            for i, lo, size in [(i, lo, size) for a, b, lo, size in blocks for i in range(a, b)]:
+                damp = jnp.broadcast_to(damping, (size, LANES))
                 old = [axl[t, k, i, lo : lo + size, :] for k in range(12)]
                 gram, n = {}, 0
                 for a in range(4):
@@ -415,7 +441,13 @@
                     sub = lax.broadcasted_iota(jnp.int32, (size, LANES), 0)
                     for k in range(12):
                         line = jnp.sum(jnp.where(lane == sub, new[k], 0.0), axis=0, keepdims=True)
-                        aligned[k // 4, k % 4, i - first : i - first + 1, :] = line[:, :cols]
+                        aligned[k // 4, k % 4, i - RING : i - RING + 1, :] = line[:, :cols]
+
+            if t + 1 < ITERS:
+                for n, (dr, dc, *_) in enumerate(edges):
+                    @pl.when(exists(dr, dc))
+                    def _():
+                        edge_copy(n).start()
 
         a = lax.broadcasted_iota(jnp.int32, (2, 2), 1)
         b = lax.broadcasted_iota(jnp.int32, (2, 2), 0)
@@ -430,6 +462,10 @@
                 tf_copy(around.index((dr, dc)), dr, dc).wait_send()
                 for copy in outer(dr, dc):
                     copy.wait_send()
+        for n, (dr, dc, *_) in enumerate(edges):
+            @pl.when(exists(dr, dc))
+            def _():
+                edge_copy(n).wait_send()
         for t in range(ITERS):
             arrived(t, got_c, n_col, c_send)
             arrived(t, got_r, n_row, r_send)
@@ -456,7 +492,7 @@
         dma((3,)), dma(()),
         dma((8, 3)), dma((8, 3)),
         dma((8,)), dma((8,)),
-        dma((ITERS,)), dma((ITERS,)), dma((ITERS,)), dma((ITERS,)),
+        dma((ITERS,)), dma((ITERS,)), dma((ITERS,)), dma((ITERS,)), dma((3,)), dma((3,)),
         pltpu.SemaphoreType.REGULAR((3,)),
     ]
     return kernel, scratch

time: 48.8 us -> 46.3 us (0.949)
  Pallas kernels: 46 us -> 43.5 us
    pallas_call x1, Pallas kernels: 46 us -> 43.5 us  [on_device(): pl.pallas_call(kernel, out_shape=(jax.ShapeDtypeStruct(transforms.shape,...]
where the time goes in v3:
time: 46.3 us; the launch traced here: 46.1 us
  Pallas kernels  43.5 us (94%)
  local copies, waits for them, and re-layouts  1.91 us (4%)
  between operations  0.65 us (1%)
    pallas_call x1, Pallas kernels, on_device(): pl.pallas_call(kernel, out_shape=(jax.ShapeDtypeStruct(transforms.shape,...  43.5 us
    unnamed x4, local copies, waits for them, and re-layouts  1.91 us

profile of v3, /device:TPU:1, one launch (start us, length us, event | category | flops | bytes accessed | tf_op | source)
XLA Modules:
  0.0 46.1 jit_solution(13209895787227044599)
XLA Ops:
  0.6 43.5 %shard_map.59 = (f32[3,4,4,16]{3,2,1,0:T(4,128)}, f32[2,2]{1,0:T(2,128)}) custom-call(f32[4,3,4,16,128]{4,3,2,1,0:T(8,128)} %here.1, f32[4,3,4,16,128]{4,3,2,1,0:T(8,128)} %there.1, s32[4,4,16,128]{3,2,1,0:T(8,128)} %mask.1, f32[3,4,4,16]{3,2,1,0:T(4,128)} %tf.1), custom_call_target="tpu_custom_call" | custom-call | tf_op jit(solution)/shard_map/pallas_call | solution.py:508
  44.2 0.0 copy-start
  44.2 1.3 %copy.8 = f32[3,4,4,16]{3,2,1,0:T(4,128)} copy(f32[3,4,4,16]{3,2,1,0:T(4,128)} %get-tuple-element.4) | data formatting | bytes 6144
  45.5 0.0 copy-done
  45.5 0.6 %copy.9 = f32[2,2]{1,0:T(2,128)} copy(f32[2,2]{1,0:T(2,128)S(1)} %copy-done) | data formatting | bytes 32
Async XLA Ops:
  44.2 1.4 %copy-start = (f32[2,2]{1,0:T(2,128)S(1)}, f32[2,2]{1,0:T(2,128)}, u32[]{:S(2)}) copy-start(f32[2,2]{1,0:T(2,128)} %get-tuple-element.5) | copy-start | bytes 52

commit v4 on v3

--- a/solution.py
+++ b/solution.py
@@ -328,7 +328,7 @@
                         sums[n, i, lo : lo + 8, :] = jnp.broadcast_to(total, (8, LANES))
                 return 0
 
-            lax.fori_loop(first, last, body, 0)
+            lax.fori_loop(first, last, body, 0, unroll=True)
 
         own[0].wait()
         for spot in ((0, 1), (0, -1), (1, 0), (1, 1), (1, -1)):
@@ -508,8 +508,8 @@
         return pl.pallas_call(
             kernel,
             out_shape=(
-                jax.ShapeDtypeStruct(transforms.shape, F32),
-                jax.ShapeDtypeStruct((2, ITERS), F32),
+                pltpu.VMEM(transforms.shape, F32),
+                pltpu.VMEM((2, ITERS), F32),
             ),
             in_specs=[hbm] * 4,
             out_specs=(pl.BlockSpec(memory_space=pltpu.VMEM),) * 2,

time: 46.3 us -> 44.4 us (0.959)
  Pallas kernels: 43.5 us -> 42.4 us
  local copies, waits for them, and re-layouts: 1.91 us -> 1.17 us
    pallas_call x1, Pallas kernels: 43.5 us -> 42.4 us  [on_device(): pl.pallas_call(kernel, out_shape=(pltpu.VMEM(transforms.shape, F32), pltp...]
    unnamed x4 -> x2, local copies, waits for them, and re-layouts: 1.91 us -> 1.17 us
where the time goes in v4:
time: 44.4 us; the launch traced here: 44.2 us
  Pallas kernels  42.4 us (95%)
  local copies, waits for them, and re-layouts  1.17 us (3%)
  between operations  0.64 us (1%)
    pallas_call x1, Pallas kernels, on_device(): pl.pallas_call(kernel, out_shape=(pltpu.VMEM(transforms.shape, F32), pltp...  42.4 us
    unnamed x2, local copies, waits for them, and re-layouts  1.17 us

profile of v4, /device:TPU:1, one launch (start us, length us, event | category | flops | bytes accessed | tf_op | source)
XLA Modules:
  0.0 44.2 jit_solution(2396759424376854174)
XLA Ops:
  0.6 42.4 %shard_map.59 = (f32[3,4,4,16]{3,2,1,0:T(4,128)S(1)}, f32[2,2]{1,0:T(2,128)S(1)}) custom-call(f32[4,3,4,16,128]{4,3,2,1,0:T(8,128)} %here.1, f32[4,3,4,16,128]{4,3,2,1,0:T(8,128)} %there.1, s32[4,4,16,128]{3,2,1,0:T(8,128)} %mask.1, f32[3,4,4,16]{3,2,1,0:T(4,128)} %tf.1), custom_call_target="tpu_custom_call" | custom-call | tf_op jit(solution)/shard_map/pallas_call | solution.py:508
  43.1 0.6 %copy.8 = f32[3,4,4,16]{3,2,1,0:T(4,128)} copy(f32[3,4,4,16]{3,2,1,0:T(4,128)S(1)} %get-tuple-element.2) | data formatting | bytes 6144
  43.7 0.6 %copy.9 = f32[2,2]{1,0:T(2,128)} copy(f32[2,2]{1,0:T(2,128)S(1)} %get-tuple-element.3) | data formatting | bytes 32

commit v5 on v4

--- a/solution.py
+++ b/solution.py
@@ -153,11 +153,42 @@
         sub8 = lax.broadcasted_iota(jnp.int32, (8, cols), 0)
         row_lane = lax.broadcasted_iota(jnp.int32, (1, LANES), 1)
 
+        own_lane = lane16 - sub8
+        picks = (
+            ((4, own_lane == -COL0), (3, own_lane == cols - COL0)),
+            ((4, own_lane == 8 - COL0),),
+            ((4, own_lane == 16 - COL0), (5, own_lane == 16 - COL0 - cols)),
+        )
+
+        def expand(i, inner=False):
+            base = 3 if 0 <= i < rows else (0 if i < 0 else 6)
+            row = i % rows
+            for k in range(12):
+                for b, pick in enumerate(picks):
+                    total = None
+                    for slot, chosen in (pick[:1] if inner else pick):
+                        line = tfv[base + slot - 3, k // 4, k % 4, row : row + 1, :]
+                        part = jnp.where(chosen, jnp.broadcast_to(line, (8, cols)), 0.0)
+                        total = part if total is None else total + part
+                    value = jnp.sum(total, axis=1, keepdims=True)
+                    axl[0, k, RING + i, 8 * b : 8 * b + 8, :] = jnp.broadcast_to(value, (8, LANES))
+
+        def column(slot, first_lane, col):
+            for k in range(12):
+                value = tfv[slot, k // 4, k % 4][:, first_lane : first_lane + 1]
+                value = jnp.broadcast_to(value, (rows, LANES))
+                for i in range(rows):
+                    axl[0, k, RING + i, COL0 + col : COL0 + col + 1, :] = value[i : i + 1, :]
+
+        own[0].wait()
+        for i in range(rows):
+            expand(i, True)
+
         pl.semaphore_wait(barrier, greeted)
 
         def tf_copy(n, dr, dc):
             return pltpu.make_async_remote_copy(
-                src_ref=tf, dst_ref=tfv.at[(1 - dr) * 3 + 1 - dc], send_sem=tf_send.at[n],
+                src_ref=tfv.at[4], dst_ref=tfv.at[(1 - dr) * 3 + 1 - dc], send_sem=tf_send.at[n],
                 recv_sem=tf_recv.at[n], device_id=(r + dr, c + dc), device_id_type=MESH)
 
         def tf_arrived(dr, dc):
@@ -167,7 +198,7 @@
             def _():
                 tf_copy(n, -dr, -dc).wait_recv()
 
-        for dr, dc in ((1, 1), (1, -1), (-1, 1), (-1, -1), (1, 0), (-1, 0), (0, 1), (0, -1)):
+        for dr, dc in ((-1, 1), (-1, -1), (-1, 0), (0, 1), (0, -1), (1, 1), (1, -1), (1, 0)):
             @pl.when(exists(dr, dc))
             def _():
                 tf_copy(around.index((dr, dc)), dr, dc).start()
@@ -234,25 +265,6 @@
         for device in (at_xy(0, 2), at_xy(0, -2), at_xy(2, 0), at_col(4), at_col(-4)):
             signal(known.at[1], device)
 
-        own_lane = lane16 - sub8
-        picks = (
-            ((4, own_lane == -COL0), (3, own_lane == cols - COL0)),
-            ((4, own_lane == 8 - COL0),),
-            ((4, own_lane == 16 - COL0), (5, own_lane == 16 - COL0 - cols)),
-        )
-
-        def expand(i):
-            base = 3 if 0 <= i < rows else (0 if i < 0 else 6)
-            row = i % rows
-            for k in range(12):
-                for b, pick in enumerate(picks):
-                    total = None
-                    for slot, chosen in pick:
-                        line = tfv[base + slot - 3, k // 4, k % 4, row : row + 1, :]
-                        part = jnp.where(chosen, jnp.broadcast_to(line, (8, cols)), 0.0)
-                        total = part if total is None else total + part
-                    value = jnp.sum(total, axis=1, keepdims=True)
-                    axl[0, k, RING + i, 8 * b : 8 * b + 8, :] = jnp.broadcast_to(value, (8, LANES))
 
         def errors(t, first, last, starts, carry=None):
             def body(i, carry):
@@ -330,11 +342,11 @@
 
             lax.fori_loop(first, last, body, 0, unroll=True)
 
-        own[0].wait()
         for spot in ((0, 1), (0, -1), (1, 0), (1, 1), (1, -1)):
             tf_arrived(*spot)
-        for i in range(rows + 1):
-            expand(i)
+        expand(rows)
+        column(3, cols - 1, -1)
+        column(5, 0, cols)
         own[2].wait()
         own[3].wait()
 
@@ -376,6 +388,8 @@
                     tf_arrived(*spot)
                 for i in (-1, rows + 1):
                     expand(i)
+                column(3, cols - 2, -2)
+                column(5, 1, cols + 1)
                 pl.semaphore_wait(known.at[2], 1)
             else:
                 for n, (dr, dc, *_) in enumerate(edges):
@@ -402,6 +416,20 @@
                 errors(t, RING - 1, RING, (1, 9, 17))
                 errors(t, RING + rows, RING + rows + 1, (1, 9, 17))
                 errors(t, RING, RING + rows, (1, 17))
+            if t + 1 == ITERS:
+                for dr, dc in around:
+                    @pl.when(exists(dr, dc))
+                    def _():
+                        tf_copy(around.index((dr, dc)), dr, dc).wait_send()
+                        for copy in outer(dr, dc):
+                            copy.wait_send()
+                for n, (dr, dc, *_) in enumerate(edges):
+                    @pl.when(exists(dr, dc))
+                    def _():
+                        edge_copy(n).wait_send()
+                arrived(0, got_c, n_col, c_send)
+                arrived(0, got_r, n_row, r_send)
+                arrived(t, got_c, n_col, c_send)
             arrived(t, got_r, n_row, r_recv)
             packed = combine(got_r[t])
             largest, total, number = packed[:, 0:1], packed[:, 32:33], packed[:, 64:65]
@@ -456,19 +484,7 @@
             jnp.where(a == 0, rec[0, 0][:, :2], rec[1, 0][:, :2]),
             jnp.where(a == 0, rec[0, 1][:, :2], rec[1, 1][:, :2]))
 
-        for dr, dc in around:
-            @pl.when(exists(dr, dc))
-            def _():
-                tf_copy(around.index((dr, dc)), dr, dc).wait_send()
-                for copy in outer(dr, dc):
-                    copy.wait_send()
-        for n, (dr, dc, *_) in enumerate(edges):
-            @pl.when(exists(dr, dc))
-            def _():
-                edge_copy(n).wait_send()
-        for t in range(ITERS):
-            arrived(t, got_c, n_col, c_send)
-            arrived(t, got_r, n_row, r_send)
+        arrived(ITERS - 1, got_r, n_row, r_send)
 
     dma = pltpu.SemaphoreType.DMA
     vm = pltpu.VMEM

time: 44.4 us -> 44 us (level)
  no operation moved by 1% of the time
where the time goes in v5:
time: 44 us; the launch traced here: 43.8 us
  Pallas kernels  42 us (95%)
  local copies, waits for them, and re-layouts  1.17 us (3%)
  between operations  0.64 us (1%)
    pallas_call x1, Pallas kernels, on_device(): pl.pallas_call(kernel, out_shape=(pltpu.VMEM(transforms.shape, F32), pltp...  42 us
    unnamed x2, local copies, waits for them, and re-layouts  1.17 us

profile of v5, /device:TPU:1, one launch (start us, length us, event | category | flops | bytes accessed | tf_op | source)
XLA Modules:
  0.0 43.8 jit_solution(12459674906868909448)
XLA Ops:
  0.6 42.0 %shard_map.59 = (f32[3,4,4,16]{3,2,1,0:T(4,128)S(1)}, f32[2,2]{1,0:T(2,128)S(1)}) custom-call(f32[4,3,4,16,128]{4,3,2,1,0:T(8,128)} %here.1, f32[4,3,4,16,128]{4,3,2,1,0:T(8,128)} %there.1, s32[4,4,16,128]{3,2,1,0:T(8,128)} %mask.1, f32[3,4,4,16]{3,2,1,0:T(4,128)} %tf.1), custom_call_target="tpu_custom_call" | custom-call | tf_op jit(solution)/shard_map/pallas_call | solution.py:524
  42.7 0.6 %copy.8 = f32[3,4,4,16]{3,2,1,0:T(4,128)} copy(f32[3,4,4,16]{3,2,1,0:T(4,128)S(1)} %get-tuple-element.2) | data formatting | bytes 6144
  43.3 0.6 %copy.9 = f32[2,2]{1,0:T(2,128)} copy(f32[2,2]{1,0:T(2,128)S(1)} %get-tuple-element.3) | data formatting | bytes 32
